TPU v7x, 32 devices: a whole 2x2x4 slice. The times are simulated.
32 devices in a mesh: dp: 8 (over y, x, core), tensor: 4 (over z).
Axes of the slice: x: 2, y: 2, z: 4, core: 2. Of those that a mesh axis runs over, the one named last changes fastest.
Arguments:
- residual: bfloat16 [4096, 4096], P(('dp', 'tensor')), may hold values from -3 to 3
- queries: bfloat16 [4096, 4096], P(('dp', 'tensor')), may hold values from -8 to 8
- rotated_key_states: bfloat16 [4096, 512], P(('dp', 'tensor')), may hold values from -8 to 8
- plain_value_states: bfloat16 [4096, 512], P(('dp', 'tensor')), may hold values from -24 to 24
- out_weight: bfloat16 [4096, 4096], P('tensor'), may hold values from -0.09375 to 0.09375
- norm_gain: bfloat16 [4096], replicated, may hold values from 0.099609375 to 1.8984375
- expert_ids: int32 [4096, 8], P(('dp', 'tensor')), may hold values from 0 to 31, all different within a row; in each aligned block of 128 rows (0 to 127, 128 to 255, ...) at most 36 rows name the same one
- gate_scales: float32 [4096, 8], P(('dp', 'tensor')), may hold values from 0.03 to 0.3
- w_gate: bfloat16 [32, 4096, 768], P(('dp', 'tensor')), may hold values from -0.09375 to 0.09375
- w_up: bfloat16 [32, 4096, 768], P(('dp', 'tensor')), may hold values from -0.09375 to 0.09375
- w_down: bfloat16 [32, 768, 4096], P(('dp', 'tensor')), may hold values from -0.21875 to 0.21875
Outputs:
- layer_out: bfloat16 [4096, 4096], P(('dp', 'tensor'))
Inputs may be any that keep to these rules, and one draw needn't show every extreme that they name: `expert_ids`: each row names 8 different experts; among the rows of one device (aligned blocks of 128 rows) no expert is named more than 36 times.
All inputs are finite; a program needn't handle non-finite values.
Results may differ from a plain program's by a relative error of at most 0.012.
Values may be sent and summed in bfloat16 or wider, within the bound.
No kernel may reach another device: no remote copies, remote signals or barrier semaphores. Data moves between devices by JAX's collectives and lax.ppermute only.
A program may use at most 192 MiB of HBM per device.

v0:
```python
import math

import jax
import jax.numpy as jnp
from jax import lax
from jax.sharding import PartitionSpec as P

D = 4096
QUERY_HEADS = 32
KEY_VALUE_HEADS = 4
HEAD_SIZE = 128
TOPK = 8


def fold_half(state, query_half, query_places, key_portion, value_portion, first_key):
    key_count = key_portion.shape[0]
    scaling = 1.0 / math.sqrt(HEAD_SIZE)

    def update(current):
        peak_old, total_old, accum_old = current
        scores = (
            jnp.einsum(
                "tkgd,nkd->kgtn", query_half, key_portion, preferred_element_type=jnp.float32
            )
            * scaling
        )
        key_places = jnp.arange(key_count, dtype=jnp.int32)
        visible = key_places[None, :] <= query_places[:, None]
        scores = jnp.where(visible, scores, -1e30)
        peak_new = jnp.maximum(peak_old, jnp.max(scores, axis=-1))
        expons = jnp.where(visible, jnp.exp(scores - peak_new[..., None]), 0.0)
        total_new = jnp.sum(expons, axis=-1)
        mixed = jnp.einsum(
            "kgtn,nkd->kgtd",
            expons.astype(jnp.bfloat16),
            value_portion,
            preferred_element_type=jnp.float32,
        )
        return (peak_new, total_new, mixed)

    return lax.cond(first_key <= jnp.max(query_places), update, lambda current: current, state)


def finish_half(state):
    peak_final, total_final, accum_final = state
    blended = accum_final / total_final[..., None]
    rows_count = blended.shape[2]
    return (
        jnp.transpose(blended, (2, 0, 1, 3))
        .reshape(rows_count, QUERY_HEADS * HEAD_SIZE)
        .astype(jnp.bfloat16)
    )


def run_expert(arrived, gate_mat, up_mat, down_mat):
    sources, slot_count, width = arrived.shape
    flat_rows = arrived.reshape(sources * slot_count, width)
    gate_part = jnp.dot(flat_rows, gate_mat, preferred_element_type=jnp.float32)
    up_part = jnp.dot(flat_rows, up_mat, preferred_element_type=jnp.float32)
    activated = (jax.nn.silu(gate_part) * up_part).astype(jnp.bfloat16)
    produced = jnp.dot(activated, down_mat, preferred_element_type=jnp.float32).astype(jnp.bfloat16)
    return produced.reshape(sources, slot_count, width)


def per_device(
    residual,
    queries,
    rotated_key_states,
    plain_value_states,
    out_weight,
    norm_gain,
    expert_ids,
    gate_scales,
    w_gate,
    w_up,
    w_down,
):
    token_row_set = residual.shape[0]
    halved_rows = token_row_set // 2
    query_group = QUERY_HEADS // KEY_VALUE_HEADS
    tensor_size = lax.axis_size("tensor")
    my_index = lax.axis_index("tensor")
    query_layout = queries.reshape(token_row_set, KEY_VALUE_HEADS, query_group, HEAD_SIZE)
    query_front = query_layout[:halved_rows]
    query_back = query_layout[halved_rows:]
    offsets = jnp.arange(halved_rows, dtype=jnp.int32)
    places_front = my_index * token_row_set + offsets
    places_back = my_index * token_row_set + halved_rows + offsets

    def empty_state():
        return (
            jnp.full((KEY_VALUE_HEADS, query_group, halved_rows), -1e30, jnp.float32),
            jnp.zeros((KEY_VALUE_HEADS, query_group, halved_rows), jnp.float32),
            jnp.zeros((KEY_VALUE_HEADS, query_group, halved_rows, HEAD_SIZE), jnp.float32),
        )

    portion_count = (
        lax.all_gather(rotated_key_states, "tensor", axis=0, tiled=True),
        lax.all_gather(plain_value_states, "tensor", axis=0, tiled=True),
    )
    first_key = jnp.int32(0)
    key_portion = portion_count[0].reshape(portion_count[0].shape[0], KEY_VALUE_HEADS, HEAD_SIZE)
    value_portion = portion_count[1].reshape(portion_count[1].shape[0], KEY_VALUE_HEADS, HEAD_SIZE)
    front_state = fold_half(
        empty_state(), query_front, places_front, key_portion, value_portion, first_key
    )
    back_state = fold_half(
        empty_state(), query_back, places_back, key_portion, value_portion, first_key
    )
    out_front = finish_half(front_state)
    out_back = finish_half(back_state)
    attended_rows = jnp.concatenate([out_front, out_back], axis=0)
    head_rows = lax.all_to_all(attended_rows, "tensor", split_axis=1, concat_axis=0, tiled=True)
    projected = lax.psum_scatter(
        jnp.dot(head_rows, out_weight, preferred_element_type=jnp.float32).astype(jnp.bfloat16),
        "tensor",
        scatter_dimension=0,
        tiled=True,
    ).astype(jnp.float32)
    hidden_state = residual.astype(jnp.float32) + projected
    inverse_rms = lax.rsqrt(jnp.mean(hidden_state * hidden_state, axis=-1, keepdims=True) + 1e-06)
    normed = (hidden_state * inverse_rms * norm_gain.astype(jnp.float32)).astype(jnp.bfloat16)
    dp_size = lax.axis_size("dp")
    expert_total = dp_size * tensor_size
    capacity = 9 * token_row_set // expert_total
    pair_total = token_row_set * TOPK
    flat_ids = expert_ids.reshape(pair_total)
    onehot = (flat_ids[:, None] == jnp.arange(expert_total, dtype=jnp.int32)[None, :]).astype(
        jnp.bfloat16
    )
    pair_places = jnp.arange(pair_total, dtype=jnp.int32)
    lower_ones = (pair_places[:, None] > pair_places[None, :]).astype(jnp.bfloat16)
    ranks = jnp.dot(lower_ones, onehot, preferred_element_type=jnp.float32)
    slots = jnp.sum(ranks * onehot.astype(jnp.float32), axis=1).astype(jnp.int32)
    target = flat_ids * capacity + slots
    owner = jnp.zeros((expert_total * capacity,), jnp.int32).at[target].set(pair_places + 1)
    source_row = jnp.where(owner > 0, (owner - 1) // TOPK, 0)
    outgoing = jnp.where((owner > 0)[:, None], normed[source_row], jnp.zeros((), jnp.bfloat16))
    outgoing = outgoing.reshape(expert_total, capacity, D)
    produced = run_expert(
        lax.all_to_all(outgoing, ("dp", "tensor"), split_axis=0, concat_axis=0, tiled=True),
        w_gate[0],
        w_up[0],
        w_down[0],
    )
    returned = lax.all_to_all(produced, ("dp", "tensor"), split_axis=0, concat_axis=0, tiled=True)
    returned_flat = returned.reshape(expert_total * capacity, D)
    picked = returned_flat[target].reshape(token_row_set, TOPK, D)
    moe_sum = jnp.sum(picked.astype(jnp.float32) * gate_scales[:, :, None], axis=1)
    return (hidden_state + moe_sum).astype(jnp.bfloat16)


def solution(mesh):
    placed = (
        P(("dp", "tensor"), None),
        P(("dp", "tensor"), None),
        P(("dp", "tensor"), None),
        P(("dp", "tensor"), None),
        P("tensor", None),
        P(),
        P(("dp", "tensor"), None),
        P(("dp", "tensor"), None),
        P(("dp", "tensor"), None, None),
        P(("dp", "tensor"), None, None),
        P(("dp", "tensor"), None, None),
    )
    return jax.shard_map(
        per_device, mesh=mesh, in_specs=placed, out_specs=P(("dp", "tensor"), None), check_vma=False
    )
```

profile of v0, /device:TPU:10, one launch (start us, length us, event | category | flops | bytes accessed | tf_op | source)
XLA Modules:
  0.0 775.5 jit_solution(9148717980520977363)
XLA Ops:
  9.0 15.5 %all_gather.6 = bf16[512,512]{0,1:T(8,128)(2,1)S(1)} all-gather(bf16[128,512]{0,1:T(8,128)(2,1)S(1)} %copy.15), channel_id=1, replica_groups=mesh['dp'=8,'tensor'=4] {'tensor'}, dimensions={0}, use_global_device_ids=true | all-gather | bytes 655360 | tf_op jit(solution)/shard_map/all_gather | solution.py:98
  25.5 14.0 %all_gather.7 = bf16[512,512]{0,1:T(8,128)(2,1)S(1)} all-gather(bf16[128,512]{0,1:T(8,128)(2,1)S(1)} %copy.16), channel_id=1, replica_groups=mesh['dp'=8,'tensor'=4] {'tensor'}, dimensions={0}, use_global_device_ids=true | all-gather | bytes 655360 | tf_op jit(solution)/shard_map/all_gather | solution.py:99
  40.2 4.8 conditional.3
  45.3 4.8 conditional.2
  50.6 24.6 %all_to_all.26 = bf16[128,4,1024]{2,0,1:T(8,128)(2,1)S(1)} all-to-all(bf16[128,4,1024]{2,0,1:T(8,128)(2,1)S(1)} %pad_maximum_fusion), channel_id=1, replica_groups=mesh['dp'=8,'tensor'=4] {'tensor'}, dimensions={1} | all-to-all | bytes 2097152 | tf_op jit(solution)/shard_map/all_to_all | solution.py:113
  75.1 9.4 %convolution_convert_fusion.1 = bf16[512,4096]{1,0:T(8,128)(2,1)} fusion(bf16[512,1024]{1,0:T(8,128)(2,1)S(1)} %bitcast.98, bf16[1024,4096]{1,0:T(8,128)(2,1)} %param.19), kind=kOutput, calls=%fused_computation.46 | convolution fusion | flops 4297064448 | bytes 13631488 | tf_op jit(solution)/shard_map/dot_general | solution.py:115
  86.2 4.3 scatter_custom_fusion
  90.7 71.1 %reduce-scatter.2.cloned.1.call-done = bf16[128,4096]{1,0:T(8,128)(2,1)} async-done(((bf16[512,4096]{1,0:T(8,128)(2,1)}), bf16[128,4096]{1,0:T(8,128)(2,1)}) %reduce-scatter.2.cloned.1.call-update) | async-done | bytes 1048592 | tf_op jit(solution)/shard_map/reduce_scatter | solution.py:114
  161.8 1.6 multiply_reduce_fusion
  165.1 7.9 %gather_fusion = bf16[1152,4096]{1,0:T(8,128)(2,1)} fusion(bf16[128,4096]{1,0:T(8,128)(2,1)S(1)} %multiply_convert_fusion, s32[2048]{0:T(1024)S(1)} %pad_clamp_fusion), kind=kCustom, calls=%fused_computation | custom fusion | bytes 18878976 | tf_op jit(solution)/shard_map/gather | solution.py:138
  173.0 13.2 %gather.9 = bf16[32,36,4096]{2,1,0:T(8,128)(2,1)} reshape(bf16[1152,4096]{1,0:T(8,128)(2,1)} %gather_fusion) | data formatting | bytes 18874368 | tf_op jit(solution)/shard_map/gather | solution.py:138
  186.2 5.6 broadcast_select_fusion
  191.8 232.1 %all_to_all.27 = bf16[32,36,4096]{2,1,0:T(8,128)(2,1)} all-to-all(bf16[32,36,4096]{2,1,0:T(8,128)(2,1)S(1)} %broadcast_select_fusion), channel_id=1, replica_groups=mesh['dp'=8,'tensor'=4] {'dp','tensor'}, dimensions={0} | all-to-all | bytes 18874368 | tf_op jit(solution)/shard_map/all_to_all | solution.py:141
  423.9 13.2 %reshape.98 = bf16[1152,4096]{1,0:T(8,128)(2,1)} reshape(bf16[32,36,4096]{2,1,0:T(8,128)(2,1)} %all_to_all.27) | data formatting | bytes 18874368 | tf_op jit(solution)/shard_map/reshape | solution.py:57
  437.1 12.0 %fusion.30 = f32[1152,768]{1,0:T(8,128)S(1)} fusion(bf16[1152,4096]{1,0:T(8,128)(2,1)} %reshape.98, bf16[1,4096,768]{2,1,0:T(8,128)(2,1)} %param.23), kind=kOutput, calls=%fused_computation.44 | convolution fusion | flops 7247757312 | bytes 19267584 | tf_op jit(solution)/shard_map/dot_general | solution.py:58
  449.2 10.3 %fusion.36 = bf16[1152,768]{1,0:T(8,128)(2,1)S(1)} fusion(bf16[1152,4096]{1,0:T(8,128)(2,1)S(1)} %copy-done.2, bf16[1,4096,768]{2,1,0:T(8,128)(2,1)} %param.24, f32[1152,768]{1,0:T(8,128)S(1)} %fusion.30), kind=kOutput, calls=%fused_computation.50 | convolution fusion | flops 7253065728 | bytes 21037056 | tf_op jit(solution)/shard_map/dot_general | solution.py:59
  459.5 9.6 %convolution_convert_fusion = bf16[1152,4096]{1,0:T(8,128)(2,1)} fusion(bf16[1152,768]{1,0:T(8,128)(2,1)S(1)} %fusion.36, bf16[1,768,4096]{2,1,0:T(8,128)(2,1)S(1)} %bitcast.105), kind=kOutput, calls=%fused_computation.39 | convolution fusion | flops 7252475904 | bytes 17498112 | tf_op jit(solution)/shard_map/dot_general | solution.py:61
  469.0 13.1 %reshape.99 = bf16[32,36,4096]{2,1,0:T(8,128)(2,1)} reshape(bf16[1152,4096]{1,0:T(8,128)(2,1)} %convolution_convert_fusion) | data formatting | bytes 18874368 | tf_op jit(solution)/shard_map/reshape | solution.py:62
  482.2 5.0 all-to-all-start.2
  487.3 231.9 %all-to-all-done.2 = bf16[32,36,4096]{2,1,0:T(8,128)(2,1)} async-done(((bf16[32,36,4096]{2,1,0:T(8,128)(2,1)}), bf16[32,36,4096]{2,1,0:T(8,128)(2,1)}, u32[]{:S(2)}, u32[]{:S(2)}) %all-to-all-start.2) | async-done | bytes 9437216 | tf_op jit(solution)/shard_map/all_to_all | solution.py:146
  719.3 13.2 %reshape.100 = bf16[1152,4096]{1,0:T(8,128)(2,1)} reshape(bf16[32,36,4096]{2,1,0:T(8,128)(2,1)} %all-to-all-done.2) | data formatting | bytes 18874368 | tf_op jit(solution)/shard_map/reshape | solution.py:147
  732.5 20.0 %gather_fusion.1 = bf16[1024,4096]{1,0:T(8,128)(2,1)} fusion(bf16[1152,4096]{1,0:T(8,128)(2,1)} %reshape.100, s32[1024]{0:T(1024)S(1)} %broadcast_clamp_fusion), kind=kCustom, calls=%fused_computation.1 | custom fusion | bytes 16781312 | tf_op jit(solution)/shard_map/gather | solution.py:148
  752.5 13.3 %fusion.26 = f32[128,4096]{1,0:T(8,128)} fusion(bf16[1024,4096]{1,0:T(8,128)(2,1)} %gather_fusion.1, f32[128,8]{1,0:T(8,128)S(1)} %copy.25), kind=kLoop, calls=%fused_computation.38 | loop fusion | flops 12058624 | bytes 10489856 | tf_op jit(solution)/shard_map/reduce_sum | solution.py:149
  765.7 2.9 add_convert_fusion
  (59 shorter events, 16.6 us)
Async XLA Ops:
  6.5 155.3 %reduce-scatter.2.cloned.1.call-start = ((), (), s32[]{:S(2)}) async-start(), calls=%async_computation.4 | async-start | bytes 5242880 | tf_op jit(solution)/shard_map/reduce_scatter | solution.py:114
  84.5 0.7 copy-start.4
  84.5 0.7 copy-start.3
  84.5 77.3 %copy-start = (bf16[128,4096]{1,0:T(8,128)(2,1)S(1)}, bf16[128,4096]{1,0:T(8,128)(2,1)}, u32[]{:S(2)}) copy-start(bf16[128,4096]{1,0:T(8,128)(2,1)} %param.15) | copy-start | bytes 3145732
  437.1 12.0 %copy-start.2 = (bf16[1152,4096]{1,0:T(8,128)(2,1)S(1)}, bf16[1152,4096]{1,0:T(8,128)(2,1)}, u32[]{:S(2)}) copy-start(bf16[1152,4096]{1,0:T(8,128)(2,1)} %reshape.98) | copy-start | bytes 28311556
  437.1 22.3 %slice-start = ((s8[6291456]{0:T(1024)(128)(4,1)}), s8[4194304]{0:T(1024)(128)(4,1)S(1)}, s32[]{:S(2)}) async-start(s8[6291456]{0:T(1024)(128)(4,1)} %bitcast.104), calls=%async_computation.5 | async-start | bytes 8388608
  449.2 10.3 %slice-start.1 = ((s8[6291456]{0:T(1024)(128)(4,1)}), s8[2097152]{0:T(1024)(128)(4,1)S(1)}, s32[]{:S(2)}) async-start(s8[6291456]{0:T(1024)(128)(4,1)} %bitcast.104), calls=%async_computation.6 | async-start | bytes 4194304
  482.2 5.0 copy-start.5
  482.2 237.1 %all-to-all-start.2 = ((bf16[32,36,4096]{2,1,0:T(8,128)(2,1)}), bf16[32,36,4096]{2,1,0:T(8,128)(2,1)}, u32[]{:S(2)}, u32[]{:S(2)}) async-start(bf16[32,36,4096]{2,1,0:T(8,128)(2,1)} %reshape.99), calls=%async_computation.3 | async-start | bytes 20971520 | tf_op jit(solution)/shard_map/all_to_all | solution.py:146
  752.5 13.3 %copy-start.1 = (bf16[128,4096]{1,0:T(8,128)(2,1)S(1)}, bf16[128,4096]{1,0:T(8,128)(2,1)}, u32[]{:S(2)}) copy-start(bf16[128,4096]{1,0:T(8,128)(2,1)} %reduce-scatter.2.cloned.1.call-done) | copy-start | bytes 3145732
Sparse Core Ops, SparseCore 0:
  84.7 77.0 reduce-scatter.1
where the time goes:
time: 778 us; the launch traced here: 776 us
  waiting for transfers between devices  303 us (39%)
  blocking collectives  286 us (37%)
  local copies, waits for them, and re-layouts  90.6 us (12%)
  matrix products  46 us (6%)
  other arithmetic  29.6 us (4%)
  between operations  15 us (2%)
    all_to_all x1, blocking collectives, per_device(): lax.all_to_all(outgoing, ('dp', 'tensor'), split_axis=0, concat_axis=0, t...  232 us
    all_to_all x1, waiting for transfers between devices, per_device(): lax.all_to_all(produced, ('dp', 'tensor'), split_axis=0, concat_axis=0, t...  232 us
    reduce_scatter x1, waiting for transfers between devices, per_device(): lax.psum_scatter(jnp.dot(head_rows, out_weight, preferred_element_type=jn...  71.1 us
    all_to_all x1, blocking collectives, per_device(): lax.all_to_all(attended_rows, 'tensor', split_axis=1, concat_axis=0, tile...  24.6 us
    gather x2, local copies, waits for them, and re-layouts, per_device(): normed[source_row]  21.1 us
    gather x1, local copies, waits for them, and re-layouts, per_device(): picked = returned_flat[target].reshape(token_row_set, TOPK, D)  20 us
  transfers between devices with their start and end apart: 2, of which 2 were waited for; matrix products, arithmetic and copies ran while one was open for 1% of the time, Pallas kernels for 0%

commit v1 on v0

v1 whole, which is shorter than its diff:
```python
import functools
import math

import jax
import jax.numpy as jnp
from jax import lax
from jax.experimental import pallas as pl
from jax.experimental.pallas import tpu as pltpu
from jax.sharding import PartitionSpec as P

D = 4096
QUERY_HEADS = 32
KEY_VALUE_HEADS = 4
HEAD_SIZE = 128
TOPK = 8


def attend_kernel(q_ref, k_ref, v_ref, o_ref, *, block):
    scaling = 1.0 / math.sqrt(HEAD_SIZE)
    total = q_ref.shape[0]
    rows = lax.broadcasted_iota(jnp.int32, (block, block), 0)
    cols = lax.broadcasted_iota(jnp.int32, (block, block), 1)
    for first in range(0, total, block):
        seen = first + block
        scores = (
            lax.dot_general(
                q_ref[first:seen, :],
                k_ref[:seen, :],
                (((1,), (1,)), ((), ())),
                preferred_element_type=jnp.float32,
            )
            * scaling
        )
        diagonal = jnp.where(cols <= rows, scores[:, first:], -1e30)
        if first:
            scores = jnp.concatenate([scores[:, :first], diagonal], axis=1)
        else:
            scores = diagonal
        peak = jnp.max(scores, axis=-1, keepdims=True)
        expons = jnp.exp(scores - peak)
        totals = jnp.sum(expons, axis=-1, keepdims=True)
        mixed = jnp.dot(
            expons.astype(jnp.bfloat16), v_ref[:seen, :], preferred_element_type=jnp.float32
        )
        o_ref[first:seen, :] = (mixed / totals).astype(jnp.bfloat16)


def attend(slab, heads):
    positions = slab.shape[0]
    return pl.pallas_call(
        functools.partial(attend_kernel, block=128),
        grid=(heads,),
        in_specs=[
            pl.BlockSpec((positions, HEAD_SIZE), lambda h: (0, h)),
            pl.BlockSpec((positions, HEAD_SIZE), lambda h: (0, heads)),
            pl.BlockSpec((positions, HEAD_SIZE), lambda h: (0, heads + 1)),
        ],
        out_specs=pl.BlockSpec((positions, HEAD_SIZE), lambda h: (0, h)),
        out_shape=jax.ShapeDtypeStruct((positions, heads * HEAD_SIZE), jnp.bfloat16),
    )(slab, slab, slab)


def run_expert(rows_in, gate_mat, up_mat, down_mat):
    gate_part = jnp.dot(rows_in, gate_mat, preferred_element_type=jnp.float32)
    up_part = jnp.dot(rows_in, up_mat, preferred_element_type=jnp.float32)
    activated = (jax.nn.silu(gate_part) * up_part).astype(jnp.bfloat16)
    return jnp.dot(activated, down_mat, preferred_element_type=jnp.float32).astype(jnp.bfloat16)


def swap(value, axis, distance, size):
    return lax.ppermute(value, axis, [(i, i ^ distance) for i in range(size)])


def exchange(rows, size):
    parted = rows.reshape(size, rows.shape[0] // size, rows.shape[1])
    parted = lax.all_to_all(parted, "dp", split_axis=0, concat_axis=0, tiled=True)
    return parted.reshape(rows.shape)


def after(*values):
    return lax.optimization_barrier(values)


def selection(ids, gates, experts, slot_count):
    match = (ids[:, :, None] == experts[None, None, :]).astype(jnp.float32)
    chosen = jnp.sum(match, axis=1)
    weight = jnp.sum(match * gates[:, :, None], axis=1)
    rows = ids.shape[0]
    order = jnp.arange(rows, dtype=jnp.int32)
    earlier = (order[:, None] > order[None, :]).astype(jnp.bfloat16)
    ranks = jnp.dot(earlier, chosen.astype(jnp.bfloat16), preferred_element_type=jnp.float32)
    slots = jnp.where(chosen > 0, ranks.astype(jnp.int32), -1)
    places = jnp.arange(slot_count, dtype=jnp.int32)
    hit = slots[:, :, None] == places[None, None, :]
    count = experts.shape[0] * slot_count
    pick = hit.astype(jnp.bfloat16).reshape(rows, count)
    blend = jnp.where(hit, weight[:, :, None], 0.0).reshape(rows, count)
    blend_high = blend.astype(jnp.bfloat16)
    blend_low = (blend - blend_high.astype(jnp.float32)).astype(jnp.bfloat16)
    return pick, blend_high, blend_low


def per_device(
    residual,
    queries,
    rotated_key_states,
    plain_value_states,
    out_weight,
    norm_gain,
    expert_ids,
    gate_scales,
    w_gate,
    w_up,
    w_down,
):
    row_count = residual.shape[0]
    tensor_size = lax.axis_size("tensor")
    dp_size = lax.axis_size("dp")
    my_tensor = lax.axis_index("tensor")
    my_dp = lax.axis_index("dp")
    heads = QUERY_HEADS // tensor_size
    shares = tensor_size // KEY_VALUE_HEADS

    routing = jnp.concatenate([expert_ids.astype(jnp.float32), gate_scales], axis=1)

    def by_head(states):
        states = states.reshape(row_count, KEY_VALUE_HEADS, HEAD_SIZE)
        return jnp.repeat(states, shares, axis=1) if shares > 1 else states

    slabs = jnp.concatenate(
        [
            queries.reshape(row_count, tensor_size, heads * HEAD_SIZE),
            by_head(rotated_key_states),
            by_head(plain_value_states),
        ],
        axis=2,
    )
    slab = lax.all_to_all(slabs, "tensor", split_axis=1, concat_axis=0, tiled=True)
    slab = slab.reshape(tensor_size * row_count, (heads + 2) * HEAD_SIZE)
    attended = attend(slab, heads)
    projected = lax.psum_scatter(
        jnp.dot(attended, out_weight, preferred_element_type=jnp.float32).astype(jnp.bfloat16),
        "tensor",
        scatter_dimension=0,
        tiled=True,
    ).astype(jnp.float32)
    hidden_state = residual.astype(jnp.float32) + projected
    inverse_rms = lax.rsqrt(jnp.mean(hidden_state * hidden_state, axis=-1, keepdims=True) + 1e-06)
    normed = (hidden_state * inverse_rms * norm_gain.astype(jnp.float32)).astype(jnp.bfloat16)

    capacity = 9 * row_count // (dp_size * tensor_size)
    experts = jnp.arange(dp_size, dtype=jnp.int32) * tensor_size + my_tensor

    slot_count = -(-capacity // 8) * 8

    def dispatch(block, plan):
        outgoing = lax.dot_general(
            plan[0], block, (((0,), (0,)), ((), ())), preferred_element_type=jnp.float32
        ).astype(jnp.bfloat16)
        return outgoing

    def combine(returned, plan):
        return jnp.dot(plan[1], returned, preferred_element_type=jnp.float32) + jnp.dot(
            plan[2], returned, preferred_element_type=jnp.float32
        )

    def expert(arrived):
        return run_expert(arrived, w_gate[0], w_up[0], w_down[0])

    def plan_for(routing):
        return selection(routing[:, :TOPK].astype(jnp.int32), routing[:, TOPK:], experts, slot_count)

    def short(value):
        return value.astype(jnp.bfloat16)

    def long(value):
        return value.astype(jnp.float32)

    if tensor_size == 4:
        pairs = [(0, 1), (1, 0), (2, 3), (3, 2)]
        middle = [(1, 2), (2, 1)]
        outward = [(1, 0), (2, 3)]
        inward = [(0, 1), (3, 2)]

        def send(value, moves):
            return lax.ppermute(value, "tensor", moves)

        def spread(block):
            near = send(block, pairs)
            inner_two = send(block, middle)
            outer_two = send(inner_two, outward)
            inner_three = send(near, middle)
            outer_three = send(inner_three, outward)
            return near, inner_two, outer_two, inner_three, outer_three

        r_near, r_in2, r_out2, r_in3, r_out3 = spread(routing)
        plans = [plan_for(r) for r in (routing, r_near, r_in2 + r_out2, r_in3 + r_out3)]

        out0 = dispatch(normed, plans[0])
        arr0 = exchange(out0, dp_size)
        source, _ = after(normed, out0)
        near = send(source, pairs)
        inner_two = send(source, middle)
        near, inner_two = after(near, inner_two)
        outer_two = send(inner_two, outward)
        inner_three = send(near, middle)
        out1 = dispatch(near, plans[1])
        arr1 = exchange(out1, dp_size)
        arr0, _ = after(arr0, out1)
        pro0 = expert(arr0)
        outer_two, inner_three, _ = after(outer_two, inner_three, pro0)
        outer_three = send(inner_three, outward)
        out2 = dispatch(inner_two + outer_two, plans[2])
        arr2 = exchange(out2, dp_size)
        arr1, _ = after(arr1, out2)
        pro1 = expert(arr1)
        outer_three, _ = after(outer_three, pro1)
        out3 = dispatch(inner_three + outer_three, plans[3])
        arr3 = exchange(out3, dp_size)
        arr2, _ = after(arr2, out3)
        pro2 = expert(arr2)
        arr3, _ = after(arr3, pro2)
        pro3 = expert(arr3)
        ret3 = exchange(pro3, dp_size)
        pro2, ret3 = after(pro2, ret3)
        ret2 = exchange(pro2, dp_size)
        part3 = short(combine(ret3, plans[3]))
        far3 = send(part3, inward)
        pro1, ret2, far3 = after(pro1, ret2, far3)
        ret1 = exchange(pro1, dp_size)
        part2 = short(combine(ret2, plans[2]))
        far2 = send(part2, inward)
        mid3 = send(short(long(part3) + long(far3)), middle)
        pro0, ret1, mid3, far2 = after(pro0, ret1, mid3, far2)
        ret0 = exchange(pro0, dp_size)
        part1 = short(combine(ret1, plans[1]) + long(mid3))
        last1 = send(part1, pairs)
        last2 = send(short(long(part2) + long(far2)), middle)
        moe_sum = combine(ret0, plans[0]) + long(last1) + long(last2)
    else:
        blocks = {0: normed}
        moe_sum = None
        for step in range(tensor_size):
            if step:
                low = step & -step
                blocks[step] = swap(blocks[step ^ low], "tensor", low, tensor_size)
            plan = plan_for(swap(routing, "tensor", step, tensor_size) if step else routing)
            arrived = exchange(dispatch(blocks[step], plan), dp_size)
            part = combine(exchange(expert(arrived), dp_size), plan)
            if step:
                part = long(swap(short(part), "tensor", step, tensor_size))
            moe_sum = part if moe_sum is None else moe_sum + part
    return (hidden_state + moe_sum).astype(jnp.bfloat16)


def solution(mesh):
    placed = (
        P(("dp", "tensor"), None),
        P(("dp", "tensor"), None),
        P(("dp", "tensor"), None),
        P(("dp", "tensor"), None),
        P("tensor", None),
        P(),
        P(("dp", "tensor"), None),
        P(("dp", "tensor"), None),
        P(("dp", "tensor"), None, None),
        P(("dp", "tensor"), None, None),
        P(("dp", "tensor"), None, None),
    )
    return jax.shard_map(
        per_device, mesh=mesh, in_specs=placed, out_specs=P(("dp", "tensor"), None), check_vma=False
    )
```

time: 778 us -> 479 us (0.62)
  blocking collectives: 286 us -> 71.4 us
  waiting for transfers between devices: 303 us -> 178 us
  local copies, waits for them, and re-layouts: 90.6 us -> 6.1 us
  starting transfers between devices: 5.03 us -> 71.1 us
  matrix products: 46 us -> 111 us
  other arithmetic: 29.6 us -> 8.75 us
  Pallas kernels: 0 us -> 11 us
    all_to_all x1 -> x7, waiting for transfers between devices: 232 us -> 30.1 us  [exchange(): lax.all_to_all(parted, 'dp', split_axis=0, concat_axis=0, tiled=True)]
    all_to_all x2, blocking collectives: 257 us -> 71.4 us  [the longest x1 36.7 us: exchange(): lax.all_to_all(parted, 'dp', split_axis=0, concat_axis=0, tiled=True)]
    ppermute x0 -> x15, waiting for transfers between devices: none -> 86.5 us  [send(): return lax.ppermute(value, 'tensor', moves)]
    gather x3 -> x0, local copies, waits for them, and re-layouts: 41 us -> none  [the longest x2 21.1 us: per_device(): normed[source_row]]
    dot_general x1 -> x4, matrix products: 9.55 us -> 49.6 us  [run_expert(): jnp.dot(activated, down_mat, preferred_element_type=jnp.float32)]
    reshape x3 -> x2, local copies, waits for them, and re-layouts: 39.6 us -> 2.29 us  [the longest x1 1.34 us: per_device(): queries.reshape(row_count, tensor_size, heads * HEAD_SIZE)]
    ppermute x0 -> x15, starting transfers between devices: none -> 36.8 us  [send(): return lax.ppermute(value, 'tensor', moves)]
    all_gather x2 -> x0, blocking collectives: 29.5 us -> none  [the longest x1 15.5 us: per_device(): lax.all_gather(rotated_key_states, 'tensor', axis=0, tiled=True)]
  transfers between devices with their start and end apart: 2 -> 23, of which waited for: 2 -> 13; matrix products, arithmetic and copies ran while one was open for 1% -> 18% of each run, Pallas kernels for 0% -> 0%
where the time goes in v1:
time: 479 us; the launch traced here: 472 us
  waiting for transfers between devices  178 us (37%)
  matrix products  111 us (23%)
  blocking collectives  71.4 us (15%)
  starting transfers between devices  71.1 us (15%)
  between operations  14.2 us (3%)
  Pallas kernels  11 us (2%)
  other arithmetic  8.75 us (2%)
  local copies, waits for them, and re-layouts  6.1 us (1%)
    ppermute x15, waiting for transfers between devices, send(): return lax.ppermute(value, 'tensor', moves)  86.5 us
    reduce_scatter x1, waiting for transfers between devices, per_device(): lax.psum_scatter(jnp.dot(attended, out_weight, preferred_element_type=jnp...  61.3 us
    dot_general x4, matrix products, run_expert(): jnp.dot(activated, down_mat, preferred_element_type=jnp.float32)  49.6 us
    ppermute x15, starting transfers between devices, send(): return lax.ppermute(value, 'tensor', moves)  36.8 us
    all_to_all x1, blocking collectives, exchange(): lax.all_to_all(parted, 'dp', split_axis=0, concat_axis=0, tiled=True)  36.7 us
    all_to_all x1, blocking collectives, per_device(): lax.all_to_all(slabs, 'tensor', split_axis=1, concat_axis=0, tiled=True)  34.8 us
    all_to_all x7, starting transfers between devices, exchange(): lax.all_to_all(parted, 'dp', split_axis=0, concat_axis=0, tiled=True)  34.3 us
    all_to_all x7, waiting for transfers between devices, exchange(): lax.all_to_all(parted, 'dp', split_axis=0, concat_axis=0, tiled=True)  30.1 us
  transfers between devices with their start and end apart: 23, of which 13 were waited for; matrix products, arithmetic and copies ran while one was open for 18% of the time, Pallas kernels for 0%

profile of v1, /device:TPU:10, one launch (start us, length us, event | category | flops | bytes accessed | tf_op | source)
XLA Modules:
  0.0 471.5 jit_solution(18216528810743817893)
XLA Ops:
  9.0 34.8 %all_to_all.55 = bf16[128,4,1280]{2,0,1:T(8,128)(2,1)} all-to-all(bf16[128,4,1280]{2,0,1:T(8,128)(2,1)S(1)} %pad_maximum_fusion), channel_id=1, replica_groups=mesh['dp'=8,'tensor'=4] {'tensor'}, dimensions={1} | all-to-all | bytes 2621440 | tf_op jit(solution)/shard_map/all_to_all | solution.py:138
  43.7 11.0 %shard_map.109 = bf16[512,1024]{1,0:T(8,128)(2,1)} custom-call(bf16[512,1280]{1,0:T(8,128)(2,1)} %bitcast.189, bf16[512,1280]{1,0:T(8,128)(2,1)} %bitcast.190, bf16[512,1280]{1,0:T(8,128)(2,1)} %bitcast.191), custom_call_target="tpu_custom_call" | custom-call | tf_op jit(solution)/shard_map/pallas_call | solution.py:50
  54.8 10.2 %convolution_convert_fusion = bf16[512,4096]{1,0:T(8,128)(2,1)} fusion(bf16[512,1024]{1,0:T(8,128)(2,1)} %shard_map.109, bf16[1024,4096]{1,0:T(8,128)(2,1)} %param.15), kind=kOutput, calls=%fused_computation.24 | convolution fusion | flops 4297064448 | bytes 13631488 | tf_op jit(solution)/shard_map/dot_general | solution.py:142
  81.1 61.3 %reduce-scatter.2.cloned.1.call-done = bf16[128,4096]{1,0:T(8,128)(2,1)} async-done(((bf16[512,4096]{1,0:T(8,128)(2,1)}), bf16[128,4096]{1,0:T(8,128)(2,1)}) %reduce-scatter.2.cloned.1.call-update) | async-done | bytes 1048592 | tf_op jit(solution)/shard_map/reduce_scatter | solution.py:141
  146.9 4.8 %all-to-all-start.1 = ((bf16[8,40,4096]{2,1,0:T(8,128)(2,1)}), bf16[8,40,4096]{2,1,0:T(8,128)(2,1)}, u32[]{:S(2)}, u32[]{:S(2)}) async-start(bf16[8,40,4096]{2,1,0:T(8,128)(2,1)} %bitcast.4), calls=%async_computation.2 | async-start | bytes 5242880 | tf_op jit(solution)/shard_map/all_to_all | solution.py:76
  156.1 20.9 %collective-permute-done.1 = bf16[128,4096]{1,0:T(8,128)(2,1)S(1)} collective-permute-done((bf16[128,4096]{1,0:T(8,128)(2,1)S(1)}, bf16[128,4096]{1,0:T(8,128)(2,1)S(1)}, u32[]{:S(2)}, u32[]{:S(2)}) %collective-permute-start.1) | collective-permute-done | bytes 1048608 | tf_op jit(solution)/shard_map/ppermute | solution.py:186
  182.7 4.9 %all-to-all-start.2 = ((bf16[8,40,4096]{2,1,0:T(8,128)(2,1)}), bf16[8,40,4096]{2,1,0:T(8,128)(2,1)S(1)}, u32[]{:S(2)}, u32[]{:S(2)}) async-start(bf16[8,40,4096]{2,1,0:T(8,128)(2,1)} %bitcast.10), calls=%async_computation.3 | async-start | bytes 5242880 | tf_op jit(solution)/shard_map/all_to_all | solution.py:76
  193.9 6.7 %fusion.22 = f32[320,768]{1,0:T(8,128)} fusion(bf16[320,4096]{1,0:T(8,128)(2,1)} %bitcast.5, bf16[1,4096,768]{2,1,0:T(8,128)(2,1)} %param.19), kind=kOutput, calls=%fused_computation.22 | convolution fusion | flops 2013265920 | bytes 9895936 | tf_op jit(solution)/shard_map/dot_general | solution.py:64
  200.7 12.8 %fusion.24 = bf16[320,4096]{1,0:T(8,128)(2,1)} fusion(bf16[1,768,4096]{2,1,0:T(8,128)(2,1)} %param.21, bf16[320,4096]{1,0:T(8,128)(2,1)} %bitcast.5, bf16[1,4096,768]{2,1,0:T(8,128)(2,1)} %param.20, f32[320,768]{1,0:T(8,128)} %fusion.22), kind=kOutput, calls=%fused_computation.25 | convolution fusion | flops 4029317120 | bytes 18808832 | tf_op jit(solution)/shard_map/dot_general | solution.py:67
  224.4 5.4 %collective-permute-start.9 = (bf16[128,4096]{1,0:T(8,128)(2,1)}, bf16[128,4096]{1,0:T(8,128)(2,1)}, u32[]{:S(2)}, u32[]{:S(2)}) collective-permute-start(bf16[128,4096]{1,0:T(8,128)(2,1)} %collective-permute-done.6), channel_id=1, source_target_pairs={{1,0},{2,3},{5,4},{6,7},{9,8},{10,11},{13,12},{14,15},{17,16},{18,... | collective-permute-start | bytes 3145736 | tf_op jit(solution)/shard_map/ppermute | solution.py:186
  229.8 5.9 %fusion.20 = f32[320,768]{1,0:T(8,128)} fusion(bf16[320,4096]{1,0:T(8,128)(2,1)S(1)} %bitcast.196, bf16[1,4096,768]{2,1,0:T(8,128)(2,1)} %param.19), kind=kOutput, calls=%fused_computation.20 | convolution fusion | flops 2013265920 | bytes 9895936 | tf_op jit(solution)/shard_map/dot_general | solution.py:64
  235.7 12.1 %fusion.27 = bf16[320,4096]{1,0:T(8,128)(2,1)} fusion(bf16[1,768,4096]{2,1,0:T(8,128)(2,1)} %param.21, bf16[320,4096]{1,0:T(8,128)(2,1)S(1)} %bitcast.197, bf16[1,4096,768]{2,1,0:T(8,128)(2,1)} %param.20, f32[320,768]{1,0:T(8,128)} %fusion.20), kind=kOutput, calls=%fused_computation.26 | convolution fusion | flops 4029317120 | bytes 18808832 | tf_op jit(solution)/shard_map/dot_general | solution.py:67
  255.7 4.8 %all-to-all-start.4 = ((bf16[8,40,4096]{2,1,0:T(8,128)(2,1)}), bf16[8,40,4096]{2,1,0:T(8,128)(2,1)S(1)}, u32[]{:S(2)}, u32[]{:S(2)}) async-start(bf16[8,40,4096]{2,1,0:T(8,128)(2,1)} %bitcast.16), calls=%async_computation.5 | async-start | bytes 5242880 | tf_op jit(solution)/shard_map/all_to_all | solution.py:76
  260.6 6.7 %fusion.18 = f32[320,768]{1,0:T(8,128)} fusion(bf16[320,4096]{1,0:T(8,128)(2,1)} %bitcast.14, bf16[1,4096,768]{2,1,0:T(8,128)(2,1)} %param.19), kind=kOutput, calls=%fused_computation.18 | convolution fusion | flops 2013265920 | bytes 9895936 | tf_op jit(solution)/shard_map/dot_general | solution.py:64
  267.3 12.7 %fusion.30 = bf16[320,4096]{1,0:T(8,128)(2,1)} fusion(bf16[1,768,4096]{2,1,0:T(8,128)(2,1)} %param.21, bf16[320,4096]{1,0:T(8,128)(2,1)} %bitcast.14, bf16[1,4096,768]{2,1,0:T(8,128)(2,1)} %param.20, f32[320,768]{1,0:T(8,128)} %fusion.18), kind=kOutput, calls=%fused_computation.27 | convolution fusion | flops 4029317120 | bytes 18808832 | tf_op jit(solution)/shard_map/dot_general | solution.py:67
  280.0 11.3 %all-to-all-done.4 = bf16[8,40,4096]{2,1,0:T(8,128)(2,1)S(1)} async-done(((bf16[8,40,4096]{2,1,0:T(8,128)(2,1)}), bf16[8,40,4096]{2,1,0:T(8,128)(2,1)S(1)}, u32[]{:S(2)}, u32[]{:S(2)}) %all-to-all-start.4) | async-done | bytes 2621472 | tf_op jit(solution)/shard_map/all_to_all | solution.py:76
  291.3 5.9 %fusion.16 = f32[320,768]{1,0:T(8,128)} fusion(bf16[320,4096]{1,0:T(8,128)(2,1)S(1)} %bitcast.198, bf16[1,4096,768]{2,1,0:T(8,128)(2,1)} %param.19), kind=kOutput, calls=%fused_computation.16 | convolution fusion | flops 2013265920 | bytes 9895936 | tf_op jit(solution)/shard_map/dot_general | solution.py:64
  297.2 12.1 %fusion.33 = bf16[320,4096]{1,0:T(8,128)(2,1)} fusion(bf16[1,768,4096]{2,1,0:T(8,128)(2,1)} %param.21, bf16[320,4096]{1,0:T(8,128)(2,1)S(1)} %bitcast.199, bf16[1,4096,768]{2,1,0:T(8,128)(2,1)} %param.20, f32[320,768]{1,0:T(8,128)} %fusion.16), kind=kOutput, calls=%fused_computation.28 | convolution fusion | flops 4029317120 | bytes 18808832 | tf_op jit(solution)/shard_map/dot_general | solution.py:67
  309.3 36.7 %all_to_all.56 = bf16[8,40,4096]{2,1,0:T(8,128)(2,1)} all-to-all(bf16[8,40,4096]{2,1,0:T(8,128)(2,1)} %bitcast.200), channel_id=1, replica_groups=mesh['dp'=8,'tensor'=4] {'dp'}, dimensions={0} | all-to-all | bytes 5242880 | tf_op jit(solution)/shard_map/all_to_all | solution.py:76
  346.0 5.3 %all-to-all-start.6 = ((bf16[8,40,4096]{2,1,0:T(8,128)(2,1)}), bf16[8,40,4096]{2,1,0:T(8,128)(2,1)S(1)}, u32[]{:S(2)}, u32[]{:S(2)}) async-start(bf16[8,40,4096]{2,1,0:T(8,128)(2,1)} %bitcast.195), calls=%async_computation.7 | async-start | bytes 5242880 | tf_op jit(solution)/shard_map/all_to_all | solution.py:76
  356.2 26.0 %collective-permute-done.10 = bf16[128,4096]{1,0:T(8,128)(2,1)} collective-permute-done((bf16[128,4096]{1,0:T(8,128)(2,1)S(1)}, bf16[128,4096]{1,0:T(8,128)(2,1)}, u32[]{:S(2)}, u32[]{:S(2)}) %collective-permute-start.10) | collective-permute-done | bytes 1048608 | tf_op jit(solution)/shard_map/ppermute | solution.py:186
  382.2 5.6 %all-to-all-start.7 = ((bf16[8,40,4096]{2,1,0:T(8,128)(2,1)}), bf16[8,40,4096]{2,1,0:T(8,128)(2,1)}, u32[]{:S(2)}, u32[]{:S(2)}) async-start(bf16[8,40,4096]{2,1,0:T(8,128)(2,1)} %bitcast.194), calls=%async_computation.8 | async-start | bytes 5242880 | tf_op jit(solution)/shard_map/all_to_all | solution.py:76
  396.9 20.7 %collective-permute-done.12 = bf16[128,4096]{1,0:T(8,128)(2,1)S(1)} collective-permute-done((bf16[128,4096]{1,0:T(8,128)(2,1)S(1)}, bf16[128,4096]{1,0:T(8,128)(2,1)S(1)}, u32[]{:S(2)}, u32[]{:S(2)}) %collective-permute-start.12) | collective-permute-done | bytes 1048608 | tf_op jit(solution)/shard_map/ppermute | solution.py:186
  436.6 18.8 %all-to-all-done.8 = bf16[8,40,4096]{2,1,0:T(8,128)(2,1)S(1)} async-done(((bf16[8,40,4096]{2,1,0:T(8,128)(2,1)}), bf16[8,40,4096]{2,1,0:T(8,128)(2,1)S(1)}, u32[]{:S(2)}, u32[]{:S(2)}) %all-to-all-start.8) | async-done | bytes 2621472 | tf_op jit(solution)/shard_map/all_to_all | solution.py:76
  (111 shorter events, 100.0 us)
Async XLA Ops:
  6.5 135.9 %reduce-scatter.2.cloned.1.call-start = ((), (), s32[]{:S(2)}) async-start(), calls=%async_computation.10 | async-start | bytes 5242880 | tf_op jit(solution)/shard_map/reduce_scatter | solution.py:141
  65.0 77.5 %copy-start.3 = (bf16[128,4096]{1,0:T(8,128)(2,1)S(1)}, bf16[128,4096]{1,0:T(8,128)(2,1)}, u32[]{:S(2)}) copy-start(bf16[128,4096]{1,0:T(8,128)(2,1)} %param.11) | copy-start | bytes 3145732
  65.7 4.5 collective-permute-start
  67.5 6.0 %collective-permute-start.3 = (f32[128,16]{0,1:T(8,128)S(1)}, f32[128,16]{0,1:T(8,128)S(1)}, u32[]{:S(2)}, u32[]{:S(2)}) collective-permute-start(f32[128,16]{0,1:T(8,128)S(1)} %pad_maximum_fusion.1), channel_id=1, source_target_pairs={{1,2},{2,1},{5,6},{6,5},{9,10},{10,9},{13,14},{14,13},{17,18},{18,... | collective-permute-start | bytes 24584 | tf_op jit(solution)/shard_map/ppermute | solution.py:186
  70.2 7.4 %collective-permute-start.7 = (f32[128,16]{0,1:T(8,128)S(1)}, f32[128,16]{0,1:T(8,128)S(1)}, u32[]{:S(2)}, u32[]{:S(2)}) collective-permute-start(f32[128,16]{0,1:T(8,128)S(1)} %collective-permute-done), channel_id=1, source_target_pairs={{1,2},{2,1},{5,6},{6,5},{9,10},{10,9},{13,14},{14,13},{17,18},{18,... | collective-permute-start | bytes 24584 | tf_op jit(solution)/shard_map/ppermute | solution.py:186
  73.5 5.3 %collective-permute-start.4 = (f32[128,16]{0,1:T(8,128)S(1)}, f32[128,16]{0,1:T(8,128)S(1)}, u32[]{:S(2)}, u32[]{:S(2)}) collective-permute-start(f32[128,16]{0,1:T(8,128)S(1)} %collective-permute-done.3), channel_id=1, source_target_pairs={{1,0},{2,3},{5,4},{6,7},{9,8},{10,11},{13,12},{14,15},{17,16},{18,... | collective-permute-start | bytes 24584 | tf_op jit(solution)/shard_map/ppermute | solution.py:186
  77.6 2.6 collective-permute-start.8
  146.9 35.8 %all-to-all-start.1 = ((bf16[8,40,4096]{2,1,0:T(8,128)(2,1)}), bf16[8,40,4096]{2,1,0:T(8,128)(2,1)}, u32[]{:S(2)}, u32[]{:S(2)}) async-start(bf16[8,40,4096]{2,1,0:T(8,128)(2,1)} %bitcast.4), calls=%async_computation.2 | async-start | bytes 5242880 | tf_op jit(solution)/shard_map/all_to_all | solution.py:76
  151.7 25.2 %collective-permute-start.1 = (bf16[128,4096]{1,0:T(8,128)(2,1)S(1)}, bf16[128,4096]{1,0:T(8,128)(2,1)S(1)}, u32[]{:S(2)}, u32[]{:S(2)}) collective-permute-start(bf16[128,4096]{1,0:T(8,128)(2,1)S(1)} %multiply_convert_fusion), channel_id=1, source_target_pairs={{0,1},{1,0},{2,3},{3,2},{4,5},{5,4},{6,7},{7,6},{8,9},{9,8},{10,11... | collective-permute-start | bytes 3145736 | tf_op jit(solution)/shard_map/ppermute | solution.py:186
  152.6 26.8 %collective-permute-start.2 = (bf16[128,4096]{1,0:T(8,128)(2,1)S(1)}, bf16[128,4096]{1,0:T(8,128)(2,1)S(1)}, u32[]{:S(2)}, u32[]{:S(2)}) collective-permute-start(bf16[128,4096]{1,0:T(8,128)(2,1)S(1)} %multiply_convert_fusion), channel_id=1, source_target_pairs={{1,2},{2,1},{5,6},{6,5},{9,10},{10,9},{13,14},{14,13},{17,18},{18,... | collective-permute-start | bytes 3145736 | tf_op jit(solution)/shard_map/ppermute | solution.py:186
  182.7 37.0 %all-to-all-start.2 = ((bf16[8,40,4096]{2,1,0:T(8,128)(2,1)}), bf16[8,40,4096]{2,1,0:T(8,128)(2,1)S(1)}, u32[]{:S(2)}, u32[]{:S(2)}) async-start(bf16[8,40,4096]{2,1,0:T(8,128)(2,1)} %bitcast.10), calls=%async_computation.3 | async-start | bytes 5242880 | tf_op jit(solution)/shard_map/all_to_all | solution.py:76
  187.7 28.2 %collective-permute-start.6 = (bf16[128,4096]{1,0:T(8,128)(2,1)}, bf16[128,4096]{1,0:T(8,128)(2,1)}, u32[]{:S(2)}, u32[]{:S(2)}) collective-permute-start(bf16[128,4096]{1,0:T(8,128)(2,1)} %copy-done.13), channel_id=1, source_target_pairs={{1,2},{2,1},{5,6},{6,5},{9,10},{10,9},{13,14},{14,13},{17,18},{18,... | collective-permute-start | bytes 3145736 | tf_op jit(solution)/shard_map/ppermute | solution.py:186
  191.5 24.3 %collective-permute-start.5 = (bf16[128,4096]{1,0:T(8,128)(2,1)}, bf16[128,4096]{1,0:T(8,128)(2,1)}, u32[]{:S(2)}, u32[]{:S(2)}) collective-permute-start(bf16[128,4096]{1,0:T(8,128)(2,1)} %copy-done.14), channel_id=1, source_target_pairs={{1,0},{2,3},{5,4},{6,7},{9,8},{10,11},{13,12},{14,15},{17,16},{18,... | collective-permute-start | bytes 3145736 | tf_op jit(solution)/shard_map/ppermute | solution.py:186
  219.7 36.0 %all-to-all-start.3 = ((bf16[8,40,4096]{2,1,0:T(8,128)(2,1)}), bf16[8,40,4096]{2,1,0:T(8,128)(2,1)}, u32[]{:S(2)}, u32[]{:S(2)}) async-start(bf16[8,40,4096]{2,1,0:T(8,128)(2,1)} %bitcast.13), calls=%async_computation.4 | async-start | bytes 5242880 | tf_op jit(solution)/shard_map/all_to_all | solution.py:76
  224.4 27.4 %collective-permute-start.9 = (bf16[128,4096]{1,0:T(8,128)(2,1)}, bf16[128,4096]{1,0:T(8,128)(2,1)}, u32[]{:S(2)}, u32[]{:S(2)}) collective-permute-start(bf16[128,4096]{1,0:T(8,128)(2,1)} %collective-permute-done.6), channel_id=1, source_target_pairs={{1,0},{2,3},{5,4},{6,7},{9,8},{10,11},{13,12},{14,15},{17,16},{18,... | collective-permute-start | bytes 3145736 | tf_op jit(solution)/shard_map/ppermute | solution.py:186
  255.7 35.5 %all-to-all-start.4 = ((bf16[8,40,4096]{2,1,0:T(8,128)(2,1)}), bf16[8,40,4096]{2,1,0:T(8,128)(2,1)S(1)}, u32[]{:S(2)}, u32[]{:S(2)}) async-start(bf16[8,40,4096]{2,1,0:T(8,128)(2,1)} %bitcast.16), calls=%async_computation.5 | async-start | bytes 5242880 | tf_op jit(solution)/shard_map/all_to_all | solution.py:76
  346.0 36.3 %all-to-all-start.6 = ((bf16[8,40,4096]{2,1,0:T(8,128)(2,1)}), bf16[8,40,4096]{2,1,0:T(8,128)(2,1)S(1)}, u32[]{:S(2)}, u32[]{:S(2)}) async-start(bf16[8,40,4096]{2,1,0:T(8,128)(2,1)} %bitcast.195), calls=%async_computation.7 | async-start | bytes 5242880 | tf_op jit(solution)/shard_map/all_to_all | solution.py:76
  354.9 27.3 %collective-permute-start.10 = (bf16[128,4096]{1,0:T(8,128)(2,1)S(1)}, bf16[128,4096]{1,0:T(8,128)(2,1)}, u32[]{:S(2)}, u32[]{:S(2)}) collective-permute-start(bf16[128,4096]{1,0:T(8,128)(2,1)S(1)} %fusion.38), channel_id=1, source_target_pairs={{0,1},{3,2},{4,5},{7,6},{8,9},{11,10},{12,13},{15,14},{16,17},{19,... | collective-permute-start | bytes 3145736 | tf_op jit(solution)/shard_map/ppermute | solution.py:186
  382.2 38.3 %all-to-all-start.7 = ((bf16[8,40,4096]{2,1,0:T(8,128)(2,1)}), bf16[8,40,4096]{2,1,0:T(8,128)(2,1)}, u32[]{:S(2)}, u32[]{:S(2)}) async-start(bf16[8,40,4096]{2,1,0:T(8,128)(2,1)} %bitcast.194), calls=%async_computation.8 | async-start | bytes 5242880 | tf_op jit(solution)/shard_map/all_to_all | solution.py:76
  390.4 27.2 %collective-permute-start.12 = (bf16[128,4096]{1,0:T(8,128)(2,1)S(1)}, bf16[128,4096]{1,0:T(8,128)(2,1)S(1)}, u32[]{:S(2)}, u32[]{:S(2)}) collective-permute-start(bf16[128,4096]{1,0:T(8,128)(2,1)S(1)} %fusion.39), channel_id=1, source_target_pairs={{0,1},{3,2},{4,5},{7,6},{8,9},{11,10},{12,13},{15,14},{16,17},{19,... | collective-permute-start | bytes 3145736 | tf_op jit(solution)/shard_map/ppermute | solution.py:186
  393.2 27.3 %collective-permute-start.11 = (bf16[128,4096]{1,0:T(8,128)(2,1)S(1)}, bf16[128,4096]{1,0:T(8,128)(2,1)}, u32[]{:S(2)}, u32[]{:S(2)}) collective-permute-start(bf16[128,4096]{1,0:T(8,128)(2,1)S(1)} %add_convert_fusion.2), channel_id=1, source_target_pairs={{1,2},{2,1},{5,6},{6,5},{9,10},{10,9},{13,14},{14,13},{17,18},{18,... | collective-permute-start | bytes 3145736 | tf_op jit(solution)/shard_map/ppermute | solution.py:186
  420.5 35.0 %all-to-all-start.8 = ((bf16[8,40,4096]{2,1,0:T(8,128)(2,1)}), bf16[8,40,4096]{2,1,0:T(8,128)(2,1)S(1)}, u32[]{:S(2)}, u32[]{:S(2)}) async-start(bf16[8,40,4096]{2,1,0:T(8,128)(2,1)} %bitcast.193), calls=%async_computation.9 | async-start | bytes 5242880 | tf_op jit(solution)/shard_map/all_to_all | solution.py:76
  431.1 25.9 %collective-permute-start.13 = (bf16[128,4096]{1,0:T(8,128)(2,1)}, bf16[128,4096]{1,0:T(8,128)(2,1)}, u32[]{:S(2)}, u32[]{:S(2)}) collective-permute-start(bf16[128,4096]{1,0:T(8,128)(2,1)} %fusion.40), channel_id=1, source_target_pairs={{0,1},{1,0},{2,3},{3,2},{4,5},{5,4},{6,7},{7,6},{8,9},{9,8},{10,11... | collective-permute-start | bytes 3145736 | tf_op jit(solution)/shard_map/ppermute | solution.py:186
  433.9 27.1 %collective-permute-start.14 = (bf16[128,4096]{1,0:T(8,128)(2,1)}, bf16[128,4096]{1,0:T(8,128)(2,1)}, u32[]{:S(2)}, u32[]{:S(2)}) collective-permute-start(bf16[128,4096]{1,0:T(8,128)(2,1)} %add_convert_fusion.1), channel_id=1, source_target_pairs={{1,2},{2,1},{5,6},{6,5},{9,10},{10,9},{13,14},{14,13},{17,18},{18,... | collective-permute-start | bytes 3145736 | tf_op jit(solution)/shard_map/ppermute | solution.py:186
  (17 other events, 52.0 us)
Sparse Core Ops, SparseCore 0:
  65.1 77.2 reduce-scatter.1
